TPU v7x, 256 devices: a whole 4x4x8 slice. The times are simulated.
256 devices in a mesh: member: 16 (over z, x_lo), lat: 8 (over y, core), lon: 2 (over x_hi).
Axes of the slice: x: 4 (x_hi: 2, x_lo: 2; x = x_hi * 2 + x_lo), y: 4, z: 8, core: 2. Of those that a mesh axis runs over, the one named last changes fastest.
Arguments:
- state: bfloat16 [100, 16, 720], P(None, 'lat', 'lon'), may hold values from -6 to 6
- target: bfloat16 [100, 16, 720], P(None, 'lat', 'lon'), may hold values from -6 to 6
- land_sea: int32 [16, 720], P('lat', 'lon'), may hold values 0 or 1
- seeds: int32 [16, 32], P('member'), may hold values from 0 to 65535
- w_in: bfloat16 [9, 100, 256], replicated, may hold values from -0.1875 to 0.1875
- w_mid: bfloat16 [9, 256, 256], replicated, may hold values from -0.125 to 0.125
- w_out: bfloat16 [100, 256], replicated, may hold values from -0.375 to 0.375
- w_noise: float32 [32, 256], replicated, may hold values from -1 to 1
Outputs:
- update_in: float32 [9, 100, 256], replicated
- update_mid: float32 [9, 256, 256], replicated
- update_out: float32 [100, 256], replicated
- update_noise: float32 [32, 256], replicated
- loss: float32 [], replicated
All inputs are finite; a program needn't handle non-finite values. No bound on the sum of `land_sea` on one device may be relied on, other than what follows from the above.
Results may differ from a plain program's by a relative error of at most 0.0014.
Values may be sent and summed in bfloat16 or wider, within the bound.
No kernel may reach another device: no remote copies, remote signals or barrier semaphores. Data moves between devices by JAX's collectives and lax.ppermute only.
A program may use at most 64 MiB of HBM per device.

v0:
```python
import jax
import jax.numpy as jnp
from jax import lax
from jax.sharding import PartitionSpec as P

SMOOTH = 0.25


def with_halo(block, sides, width):
    for axis, dim in sides:
        count = lax.axis_size(axis)
        forward = [(i, i + 1) for i in range(count - 1)]
        forward.append((count - 1, 0))
        backward = [(target, source) for source, target in forward]
        low = lax.ppermute(
            lax.slice_in_dim(block, block.shape[dim] - width, None, axis=dim), axis, forward
        )
        high = lax.ppermute(lax.slice_in_dim(block, 0, width, axis=dim), axis, backward)
        block = jnp.concatenate([low, block, high], axis=dim)
    return block


def shifted(padded, offset, row_count, col_count):
    row_shift = offset // 3
    col_shift = offset % 3
    window = padded[:, row_shift : row_shift + row_count, col_shift : col_shift + col_count]
    return window.reshape(padded.shape[0], row_count * col_count)


def conv_forward(weights, padded, row_count, col_count):
    summed = None
    for offset in range(9):
        window = shifted(padded, offset, row_count, col_count)
        part = lax.dot_general(
            weights[offset], window, (((0,), (0,)), ((), ())), preferred_element_type=jnp.float32
        )
        summed = part if summed is None else summed + part
    return summed


def conv_back(weights, padded, row_count, col_count):
    summed = None
    for offset in range(9):
        window = shifted(padded, 8 - offset, row_count, col_count)
        part = jnp.dot(weights[offset], window, preferred_element_type=jnp.float32)
        summed = part if summed is None else summed + part
    return summed


def weight_grad(padded, deltas, row_count, col_count):
    parts = []
    for offset in range(9):
        window = shifted(padded, offset, row_count, col_count)
        parts.append(
            lax.dot_general(
                window, deltas, (((1,), (1,)), ((), ())), preferred_element_type=jnp.float32
            )
        )
    return jnp.stack(parts)


def gelu_pair(pre):
    return jax.jvp(jax.nn.gelu, (pre,), (jnp.ones_like(pre),))


def clear_outside(padded, width, lat_index, lat_count):
    row_count = padded.shape[1] - 2 * width
    global_row = lat_index * row_count + jnp.arange(padded.shape[1], dtype=jnp.int32) - width
    inside = (global_row >= 0) & (global_row < row_count * lat_count)
    return jnp.where(inside[None, :, None], padded, jnp.zeros((), padded.dtype))


def combine(outputs, target_flat, weights, slope_sum, spread_sum, members):
    misses = outputs - target_flat[None]
    radius = jnp.sqrt(misses * misses + SMOOTH * SMOOTH)
    gradients = weights[None] * (misses / radius / members - slope_sum / (members * (members - 1)))
    loss_term = jnp.sum(
        weights[None] * ((radius - SMOOTH) / members - spread_sum / (2 * members * (members - 1)))
    )
    return (gradients, loss_term)


def pair_sums(outputs, others, running):

    def add_member(totals, member_out):
        gap_value = outputs - member_out.astype(jnp.float32)[None]
        radius = jnp.sqrt(gap_value * gap_value + SMOOTH * SMOOTH)
        return ((totals[0] + gap_value / radius, totals[1] + radius - SMOOTH), None)

    sums, _ = lax.scan(add_member, running, others)
    return sums


def normalize(gradient):
    return gradient / jnp.sqrt(jnp.mean(gradient * gradient) + 1e-06)


def body(state, target, land_sea, seeds, w_in, w_mid, w_out, w_noise):
    variables, row_count, col_count = state.shape
    channels = w_in.shape[2]
    cell_count = row_count * col_count
    lat_index = lax.axis_index("lat")
    lat_count = lax.axis_size("lat")
    members = lax.axis_size("member")
    latent = (seeds[0].astype(jnp.float32) - 32767.5) / 18918.0
    noise_bias = jnp.dot(latent, w_noise, precision=lax.Precision.HIGHEST)
    state_wide = with_halo(state, (("lat", 1), ("lon", 2)), 2)
    state_wide = clear_outside(state_wide, 2, lat_index, lat_count)
    pre_ext = conv_forward(w_in, state_wide, row_count + 2, col_count + 2) + noise_bias[:, None]
    act_ext, slope_ext = gelu_pair(pre_ext)
    hidden_pad = act_ext.astype(jnp.bfloat16).reshape(channels, row_count + 2, col_count + 2)
    hidden_pad = clear_outside(hidden_pad, 1, lat_index, lat_count)
    state_pad = state_wide[:, 1:-1, 1:-1]
    slope_in = slope_ext.reshape(channels, row_count + 2, col_count + 2)[:, 1:-1, 1:-1].reshape(
        channels, cell_count
    )
    hidden_in = hidden_pad[:, 1:-1, 1:-1].reshape(channels, cell_count)
    pre_mid = conv_forward(w_mid, hidden_pad, row_count, col_count)
    act_mid, slope_mid = gelu_pair(pre_mid)
    hidden_out = (act_mid + hidden_in.astype(jnp.float32)).astype(jnp.bfloat16)
    flat_state = state.reshape(variables, cell_count).astype(jnp.float32)
    output = (flat_state + jnp.dot(w_out, hidden_out, preferred_element_type=jnp.float32)).astype(
        jnp.bfloat16
    )
    target_flat = target.reshape(variables, cell_count).astype(jnp.float32)
    weights = 1.0 + land_sea.reshape(1, cell_count).astype(jnp.float32)
    share_cells = cell_count // members
    gathered = lax.all_to_all(output[None], "member", split_axis=2, concat_axis=0, tiled=True)
    first_cell = lax.axis_index("member") * share_cells
    own_target = lax.dynamic_slice_in_dim(target_flat, first_cell, share_cells, 1)
    own_weights = lax.dynamic_slice_in_dim(weights, first_cell, share_cells, 1)
    gathered_f = gathered.astype(jnp.float32)
    blank = jnp.zeros(gathered_f.shape, jnp.float32)
    slope_sum, spread_sum = pair_sums(gathered_f, gathered, (blank, blank))
    gradients, loss_term = combine(
        gathered_f, own_target, own_weights, slope_sum, spread_sum, members
    )
    returned = lax.all_to_all(
        gradients.astype(jnp.bfloat16), "member", split_axis=0, concat_axis=2, tiled=True
    )
    delta_out = returned[0]
    grad_out = lax.dot_general(
        delta_out, hidden_out, (((1,), (1,)), ((), ())), preferred_element_type=jnp.float32
    )
    upstream = lax.dot_general(
        w_out, delta_out, (((0,), (0,)), ((), ())), preferred_element_type=jnp.float32
    )
    delta_mid = (upstream * slope_mid).astype(jnp.bfloat16)
    delta_pad = with_halo(
        delta_mid.reshape(channels, row_count, col_count), (("lat", 1), ("lon", 2)), 1
    )
    delta_pad = clear_outside(delta_pad, 1, lat_index, lat_count)
    incoming = conv_back(w_mid, delta_pad, row_count, col_count) + upstream
    delta_in = (incoming * slope_in).astype(jnp.bfloat16)
    grad_mid = weight_grad(hidden_pad, delta_mid, row_count, col_count)
    grad_in = weight_grad(state_pad, delta_in, row_count, col_count)
    grad_noise = latent[:, None] * jnp.sum(delta_in.astype(jnp.float32), axis=1)[None, :]
    grad_in, grad_mid, grad_out, grad_noise, summed = lax.psum(
        (grad_in, grad_mid, grad_out, grad_noise, loss_term), ("member", "lat", "lon")
    )
    loss = summed / (variables * cell_count * lat_count * lax.axis_size("lon"))
    return (
        normalize(grad_in),
        normalize(grad_mid),
        normalize(grad_out),
        normalize(grad_noise),
        loss,
    )


def solution(mesh):
    placed = (
        P(None, "lat", "lon"),
        P(None, "lat", "lon"),
        P("lat", "lon"),
        P("member", None),
        P(),
        P(),
        P(),
        P(),
    )
    return jax.shard_map(
        body, mesh=mesh, in_specs=placed, out_specs=(P(), P(), P(), P(), P()), check_vma=False
    )
```

profile of v0, /device:TPU:8, one launch (start us, length us, event | category | flops | bytes accessed | tf_op | source)
XLA Modules:
  0.0 410.6 jit_solution(16598785984211095864)
XLA Ops:
  7.2 1.7 collective-permute-start.1
  9.0 0.9 fusion.108
  9.9 2.2 collective-permute-done
  12.1 1.3 pad_maximum_fusion.2
  13.4 3.1 collective-permute-start.2
  17.0 1.0 reshape.240
  18.0 4.2 %collective-permute-done.2 = bf16[100,6,2]{2,1,0:T(8,128)(2,1)S(1)} collective-permute-done((bf16[100,6,2]{2,1,0:T(8,128)(2,1)S(1)}, bf16[100,6,2]{2,1,0:T(8,128)(2,1)S(1)}, u32[]{:S(2)}, u32[]{:S(2)}) %collective-permute-start.2) | collective-permute-done | bytes 2432 | tf_op jit(solution)/shard_map/ppermute | solution.py:15
  22.2 4.4 %collective-permute-done.3 = bf16[100,6,2]{2,1,0:T(8,128)(2,1)S(1)} collective-permute-done((bf16[100,6,2]{2,1,0:T(8,128)(2,1)S(1)}, bf16[100,6,2]{2,1,0:T(8,128)(2,1)S(1)}, u32[]{:S(2)}, u32[]{:S(2)}) %collective-permute-start.3) | collective-permute-done | bytes 2432 | tf_op jit(solution)/shard_map/ppermute | solution.py:18
  26.6 1.3 maximum_select_fusion.1
  27.9 2.1 fusion.116
  31.9 1.3 reshape.207
  33.2 2.0 reshape.208
  35.2 1.3 fusion.97
  39.8 2.4 multiply_convert_fusion
  42.9 0.8 copy-done.2
  45.9 1.3 add_convert_fusion
  47.3 0.7 copy-done.21
  48.3 1.1 copy.20
  49.9 1.9 reduce.2
  51.8 0.9 reshape.246
  52.6 9.5 %all-to-all-start = ((bf16[16,2,2250]{2,1,0:T(2,128)(2,1)}), bf16[16,2,2250]{2,1,0:T(2,128)(2,1)S(1)}, u32[]{:S(2)}, u32[]{:S(2)}) async-start(bf16[16,2,2250]{2,1,0:T(2,128)(2,1)} %reshape.246), calls=%async_computation | async-start | bytes 294912 | tf_op jit(solution)/shard_map/all_to_all | solution.py:128
  62.5 2.7 reshape.229
  65.2 2.0 slice.303
  67.2 5.4 %all-to-all-done = bf16[16,2,2250]{2,1,0:T(2,128)(2,1)S(1)} async-done(((bf16[16,2,2250]{2,1,0:T(2,128)(2,1)}), bf16[16,2,2250]{2,1,0:T(2,128)(2,1)S(1)}, u32[]{:S(2)}, u32[]{:S(2)}) %all-to-all-start) | async-done | bytes 144032 | tf_op jit(solution)/shard_map/all_to_all | solution.py:128
  73.0 1.1 bitcast_reduce_fusion
  74.1 0.8 bitcast_convert_fusion.1
  74.9 1.3 copy.23
  76.2 12.8 %while.15 = (s32[]{:T(128)}, f32[16,100,45]{2,1,0:T(8,128)S(1)}, f32[16,100,45]{2,1,0:T(8,128)S(1)}, bf16[16,100,45]{1,2,0:T(8,128)(2,1)S(1)}, f32[16,100,45]{2,1,0:T(8,128)S(1)}, /*index=5*/s32[]{:T(128)}, s32[]{:T(128)}) while((s32[]{:T(128)}, f32[16,100,45]{2,1,0:T(8,128)S(1)}, f32[16,100,45]{2,1,0:T(8,128)S(1)}, ...), condition=%wide.region_1.2_spmd.clone, body=%wide.region_0.1_spmd.clone.sunk | while | flops 652503 | bytes 1521091 | solution.py:90
  89.7 1.6 multiply_reduce_fusion.2
  91.3 3.5 all-to-all-start.1
  94.9 1.7 fusion.115
  98.1 7.0 %all-to-all-done.1 = bf16[16,100,45]{1,2,0:T(8,128)(2,1)S(1)} async-done(((bf16[16,100,45]{1,2,0:T(8,128)(2,1)}), bf16[16,100,45]{1,2,0:T(8,128)(2,1)S(1)}, u32[]{:S(2)}, u32[]{:S(2)}) %all-to-all-start.1) | async-done | bytes 144032 | tf_op jit(solution)/shard_map/all_to_all | solution.py:138
  106.5 1.7 collective-permute-start.5
  111.5 3.0 collective-permute-start.6
  114.5 0.8 collective-permute-start.7
  115.3 0.9 fusion.118
  116.9 2.7 collective-permute-done.7
  120.4 0.9 copy-done.3
  123.6 0.8 copy-done.19
  126.8 0.9 copy-done.28
  127.8 75.6 %all-reduce = (f32[32,256]{1,0:T(8,128)S(1)}, f32[]{:T(128)}) all-reduce(f32[32,256]{1,0:T(8,128)S(1)} %broadcast_multiply_fusion, f32[]{:T(128)} %get-tuple-element.162), channel_id=1, replica_groups=mesh['member'=16,'lat'=8,'lon'=2] {'member','lat','lon'}, use_global_device_ids=true, to_apply=%region_9.10 | all-reduce | flops 8193 | bytes 65544 | tf_op jit(solution)/shard_map/psum | solution.py:158
  206.0 185.0 %all-reduce.4.cloned.1.call-done = (f32[9,100,256]{2,1,0:T(8,128)}, f32[9,256,256]{2,1,0:T(8,128)}, f32[100,256]{1,0:T(8,128)}) async-done(((f32[9,100,256]{2,1,0:T(8,128)}, f32[9,256,256]{2,1,0:T(8,128)}, f32[100,256]{1,0:T(8,128)}), (f32[9,100,256]{2,1,0:T(8,128)}, f32[9,256,256]{2,1,0:T(8,128)}, f32[100,256]{1,0:T(8,128)})) %all-reduce.4.cloned.1.call-update) | async-done | bytes 3383312 | tf_op jit(solution)/shard_map/psum | solution.py:158
  390.9 1.7 multiply_reduce_fusion.3
  393.3 1.6 broadcast_divide_fusion.2
  394.9 2.9 multiply_reduce_fusion
  398.5 1.6 broadcast_divide_fusion
  400.1 0.8 multiply_reduce_fusion.1
  401.6 1.0 broadcast_divide_fusion.1
  (224 shorter events, 36.1 us)
Async XLA Ops:
  7.2 40.8 %copy-start = (bf16[100,256]{1,0:T(8,128)(2,1)S(1)}, bf16[100,256]{1,0:T(8,128)(2,1)}, u32[]{:S(2)}) copy-start(bf16[100,256]{1,0:T(8,128)(2,1)} %param.16) | copy-start | bytes 153604
  7.2 19.5 %copy-start.27 = (bf16[100,2,360]{2,1,0:T(2,128)(2,1)S(1)}, bf16[100,2,360]{2,1,0:T(2,128)(2,1)}, u32[]{:S(2)}) copy-start(bf16[100,2,360]{2,1,0:T(2,128)(2,1)} %param.10) | copy-start | bytes 432004
  7.2 4.9 %collective-permute-start = (bf16[100,2,360]{2,1,0:T(2,128)(2,1)}, bf16[100,2,360]{2,1,0:T(2,128)(2,1)S(1)}, u32[]{:S(2)}, u32[]{:S(2)}) collective-permute-start(bf16[100,2,360]{2,1,0:T(2,128)(2,1)} %param.10), channel_id=1, source_target_pairs={{0,2},{2,4},{4,6},{6,8},{8,10},{10,12},{12,14},{14,0},{1,3},{3,5},... | collective-permute-start | bytes 432008 | tf_op jit(solution)/shard_map/ppermute | solution.py:15
  7.2 4.8 %collective-permute-start.1 = (bf16[100,2,360]{2,1,0:T(2,128)(2,1)}, bf16[100,2,360]{2,1,0:T(2,128)(2,1)S(1)}, u32[]{:S(2)}, u32[]{:S(2)}) collective-permute-start(bf16[100,2,360]{2,1,0:T(2,128)(2,1)} %param.10), channel_id=1, source_target_pairs={{2,0},{4,2},{6,4},{8,6},{10,8},{12,10},{14,12},{0,14},{3,1},{5,3},... | collective-permute-start | bytes 432008 | tf_op jit(solution)/shard_map/ppermute | solution.py:18
  13.4 8.9 %collective-permute-start.2 = (bf16[100,6,2]{2,1,0:T(8,128)(2,1)S(1)}, bf16[100,6,2]{2,1,0:T(8,128)(2,1)S(1)}, u32[]{:S(2)}, u32[]{:S(2)}) collective-permute-start(bf16[100,6,2]{2,1,0:T(8,128)(2,1)S(1)} %get-tuple-element.158), channel_id=1, source_target_pairs={{0,1},{1,0},{2,3},{3,2},{4,5},{5,4},{6,7},{7,6},{8,9},{9,8},{10,11... | collective-permute-start | bytes 7208 | tf_op jit(solution)/shard_map/ppermute | solution.py:15
  16.5 10.1 %collective-permute-start.3 = (bf16[100,6,2]{2,1,0:T(8,128)(2,1)S(1)}, bf16[100,6,2]{2,1,0:T(8,128)(2,1)S(1)}, u32[]{:S(2)}, u32[]{:S(2)}) collective-permute-start(bf16[100,6,2]{2,1,0:T(8,128)(2,1)S(1)} %get-tuple-element.159), channel_id=1, source_target_pairs={{1,0},{0,1},{3,2},{2,3},{5,4},{4,5},{7,6},{6,7},{9,8},{8,9},{11,10... | collective-permute-start | bytes 7208 | tf_op jit(solution)/shard_map/ppermute | solution.py:18
  35.2 1.3 copy-start.29
  38.8 1.0 copy-start.30
  42.5 1.3 copy-start.2
  42.8 1.4 copy-start.17
  42.8 1.4 copy-start.23
  42.8 1.4 copy-start.15
  42.8 1.7 copy-start.13
  42.8 2.2 copy-start.9
  42.9 2.5 copy-start.7
  42.9 2.7 copy-start.5
  42.9 3.0 copy-start.11
  42.9 3.0 copy-start.25
  47.3 0.7 copy-start.21
  47.3 14.9 %copy-start.32 = (s32[2,360]{1,0:T(2,128)S(1)}, s32[2,360]{1,0:T(2,128)}, u32[]{:S(2)}) copy-start(s32[2,360]{1,0:T(2,128)} %param.12) | copy-start | bytes 8644
  47.3 14.9 %copy-start.31 = (bf16[100,2,360]{2,1,0:T(2,128)(2,1)S(1)}, bf16[100,2,360]{2,1,0:T(2,128)(2,1)}, u32[]{:S(2)}) copy-start(bf16[100,2,360]{2,1,0:T(2,128)(2,1)} %param.11) | copy-start | bytes 432004
  52.6 20.0 %all-to-all-start = ((bf16[16,2,2250]{2,1,0:T(2,128)(2,1)}), bf16[16,2,2250]{2,1,0:T(2,128)(2,1)S(1)}, u32[]{:S(2)}, u32[]{:S(2)}) async-start(bf16[16,2,2250]{2,1,0:T(2,128)(2,1)} %reshape.246), calls=%async_computation | async-start | bytes 294912 | tf_op jit(solution)/shard_map/all_to_all | solution.py:128
  91.3 13.7 %all-to-all-start.1 = ((bf16[16,100,45]{1,2,0:T(8,128)(2,1)}), bf16[16,100,45]{1,2,0:T(8,128)(2,1)S(1)}, u32[]{:S(2)}, u32[]{:S(2)}) async-start(bf16[16,100,45]{1,2,0:T(8,128)(2,1)} %get-tuple-element.163), calls=%async_computation.1 | async-start | bytes 393216 | tf_op jit(solution)/shard_map/all_to_all | solution.py:138
  94.9 296.1 %all-reduce.4.cloned.1.call-start = ((), (), s32[]{:S(2)}) async-start(), calls=%async_computation.2 | async-start | bytes 6848512 | tf_op jit(solution)/shard_map/psum | solution.py:158
  96.8 8.3 %copy-start.34 = (f32[256,720]{0,1:T(8,128)S(1)}, f32[256,720]{0,1:T(8,128)}, u32[]{:S(2)}) copy-start(f32[256,720]{0,1:T(8,128)} %get-tuple-element.165) | copy-start | bytes 2211844
  105.2 1.0 copy-start.24
  105.7 2.6 copy-start.18
  105.7 2.9 copy-start.16
  106.5 2.5 copy-start.14
  106.5 5.0 %collective-permute-start.4 = (bf16[256,1,360]{0,2,1:T(8,128)(2,1)S(1)}, bf16[256,1,360]{0,2,1:T(8,128)(2,1)S(1)}, u32[]{:S(2)}, u32[]{:S(2)}) collective-permute-start(bf16[256,1,360]{0,2,1:T(8,128)(2,1)S(1)} %get-tuple-element.160), channel_id=1, source_target_pairs={{0,2},{2,4},{4,6},{6,8},{8,10},{10,12},{12,14},{14,0},{1,3},{3,5},... | collective-permute-start | bytes 552968 | tf_op jit(solution)/shard_map/ppermute | solution.py:15
  106.5 2.7 copy-start.12
  106.5 4.9 %collective-permute-start.5 = (bf16[256,1,360]{0,2,1:T(8,128)(2,1)S(1)}, bf16[256,1,360]{0,2,1:T(8,128)(2,1)S(1)}, u32[]{:S(2)}, u32[]{:S(2)}) collective-permute-start(bf16[256,1,360]{0,2,1:T(8,128)(2,1)S(1)} %get-tuple-element.161), channel_id=1, source_target_pairs={{2,0},{4,2},{6,4},{8,6},{10,8},{12,10},{14,12},{0,14},{3,1},{5,3},... | collective-permute-start | bytes 552968 | tf_op jit(solution)/shard_map/ppermute | solution.py:18
  108.6 1.0 copy-start.10
  108.9 1.0 copy-start.8
  109.3 1.0 copy-start.6
  109.6 1.0 copy-start.26
  110.3 5.0 %copy-start.22 = (bf16[256,720]{0,1:T(8,128)(2,1)S(1)}, bf16[256,720]{0,1:T(8,128)(2,1)}, u32[]{:S(2)}) copy-start(bf16[256,720]{0,1:T(8,128)(2,1)} %copy-done.21) | copy-start | bytes 1105924
  111.0 9.4 %copy-start.20 = (f32[9,256,256]{2,1,0:T(8,128)}, f32[9,256,256]{2,1,0:T(8,128)S(1)}, u32[]{:S(2)}) copy-start(f32[9,256,256]{2,1,0:T(8,128)S(1)} %fusion.19) | copy-start | bytes 7077892
  111.5 5.4 %collective-permute-start.6 = (bf16[256,4,1]{0,2,1:T(2,128)(2,1)S(1)}, bf16[256,4,1]{0,2,1:T(2,128)(2,1)S(1)}, u32[]{:S(2)}, u32[]{:S(2)}) collective-permute-start(bf16[256,4,1]{0,2,1:T(2,128)(2,1)S(1)} %get-tuple-element.138), channel_id=1, source_target_pairs={{0,1},{1,0},{2,3},{3,2},{4,5},{5,4},{6,7},{7,6},{8,9},{9,8},{10,11... | collective-permute-start | bytes 6152 | tf_op jit(solution)/shard_map/ppermute | solution.py:15
  114.5 5.1 %collective-permute-start.7 = (bf16[256,4,1]{0,2,1:T(2,128)(2,1)S(1)}, bf16[256,4,1]{0,2,1:T(2,128)(2,1)S(1)}, u32[]{:S(2)}, u32[]{:S(2)}) collective-permute-start(bf16[256,4,1]{0,2,1:T(2,128)(2,1)S(1)} %get-tuple-element.139), channel_id=1, source_target_pairs={{1,0},{0,1},{3,2},{2,3},{5,4},{4,5},{7,6},{6,7},{9,8},{8,9},{11,10... | collective-permute-start | bytes 6152 | tf_op jit(solution)/shard_map/ppermute | solution.py:18
  120.0 1.3 copy-start.3
  123.3 1.1 copy-start.19
  126.8 0.9 copy-start.28
  126.8 1.0 copy-start.33
  390.9 7.5 %copy-start.1 = (f32[9,256,256]{2,1,0:T(8,128)S(1)}, f32[9,256,256]{2,1,0:T(8,128)}, u32[]{:S(2)}) copy-start(f32[9,256,256]{2,1,0:T(8,128)} %get-tuple-element.114) | copy-start | bytes 7077892
  398.5 1.6 copy-start.4
Sparse Core Ops, SparseCore 0:
  127.8 263.0 all-reduce.3
where the time goes:
time: 412 us; the launch traced here: 411 us
  waiting for transfers between devices  212 us (51%)
  blocking collectives  75.6 us (18%)
  local copies, waits for them, and re-layouts  30.9 us (8%)
  other arithmetic  28.4 us (7%)
  starting transfers between devices  24 us (6%)
  matrix products  19.6 us (5%)
  between operations  19.6 us (5%)
    psum x1, waiting for transfers between devices, body(): lax.psum((grad_in, grad_mid, grad_out, grad_noise, loss_term), ('member',...  185 us
    psum x1, blocking collectives, body(): lax.psum((grad_in, grad_mid, grad_out, grad_noise, loss_term), ('member',...  75.6 us
    sub x16, other arithmetic, add_member(): return ((totals[0] + gap_value / radius, totals[1] + radius - SMOOTH), None)  10 us
    dot_general x18, matrix products, conv_forward(): lax.dot_general(weights[offset], window, (((0,), (0,)), ((), ())), prefer...  9.69 us
    all_to_all x1, starting transfers between devices, body(): lax.all_to_all(output[None], 'member', split_axis=2, concat_axis=0, tiled...  9.48 us
    unnamed x74, local copies, waits for them, and re-layouts  8.47 us
  transfers between devices with their start and end apart: 11, of which 9 were waited for; matrix products, arithmetic and copies ran while one was open for 4% of the time, Pallas kernels for 0%

commit v1 on v0

--- a/solution.py
+++ b/solution.py
@@ -4,6 +4,10 @@
 from jax.sharding import PartitionSpec as P
 
 SMOOTH = 0.25
+
+
+def touch_quarters_in(vector):
+    return jax.lax.psum(jax.lax.psum(vector, axis_name="member"), axis_name=("lat", "lon"))
 
 
 def with_halo(block, sides, width):
@@ -155,8 +159,8 @@
     grad_mid = weight_grad(hidden_pad, delta_mid, row_count, col_count)
     grad_in = weight_grad(state_pad, delta_in, row_count, col_count)
     grad_noise = latent[:, None] * jnp.sum(delta_in.astype(jnp.float32), axis=1)[None, :]
-    grad_in, grad_mid, grad_out, grad_noise, summed = lax.psum(
-        (grad_in, grad_mid, grad_out, grad_noise, loss_term), ("member", "lat", "lon")
+    grad_in, grad_mid, grad_out, grad_noise, summed = touch_quarters_in(
+        (grad_in, grad_mid, grad_out, grad_noise, loss_term)
     )
     loss = summed / (variables * cell_count * lat_count * lax.axis_size("lon"))
     return (

time: 412 us -> 502 us (1.22)
  blocking collectives: 75.6 us -> 132 us
  waiting for transfers between devices: 212 us -> 243 us
    psum x1 -> x2, blocking collectives: 75.6 us -> 132 us  [the longest x1 66.2 us: touch_quarters_in(): jax.lax.psum(vector, axis_name='member')]
    psum x1 -> x2, waiting for transfers between devices: 185 us -> 216 us  [the longest x1 171 us: touch_quarters_in(): jax.lax.psum(vector, axis_name='member')]
  transfers between devices with their start and end apart: 11 -> 12, of which waited for: 9 -> 10; matrix products, arithmetic and copies ran while one was open for 4% -> 3% of each run, Pallas kernels for 0% -> 0%
where the time goes in v1:
time: 502 us; the launch traced here: 499 us
  waiting for transfers between devices  243 us (48%)
  blocking collectives  132 us (26%)
  local copies, waits for them, and re-layouts  31.5 us (6%)
  other arithmetic  28.4 us (6%)
  starting transfers between devices  24 us (5%)
  matrix products  19.6 us (4%)
  between operations  19.6 us (4%)
    psum x1, waiting for transfers between devices, touch_quarters_in(): jax.lax.psum(vector, axis_name='member')  171 us
    psum x1, blocking collectives, touch_quarters_in(): jax.lax.psum(vector, axis_name='member')  66.2 us
    psum x1, blocking collectives, touch_quarters_in(): jax.lax.psum(jax.lax.psum(vector, axis_name='member'), axis_name=('lat',...  66.1 us
    psum x1, waiting for transfers between devices, touch_quarters_in(): jax.lax.psum(jax.lax.psum(vector, axis_name='member'), axis_name=('lat',...  45.4 us
  transfers between devices with their start and end apart: 12, of which 10 were waited for; matrix products, arithmetic and copies ran while one was open for 3% of the time, Pallas kernels for 0%

profile of v1, /device:TPU:8, one launch (start us, length us, event | category | flops | bytes accessed | tf_op | source)
XLA Modules:
  0.0 499.2 jit_solution(3338643058337533611)
XLA Ops:
  7.2 1.7 collective-permute-start.1
  9.0 0.9 fusion.108
  9.9 2.2 collective-permute-done
  12.1 1.3 pad_maximum_fusion.2
  13.4 3.1 collective-permute-start.2
  17.0 1.0 reshape.240
  18.0 4.2 collective-permute-done.2
  22.2 4.4 collective-permute-done.3
  26.6 1.3 maximum_select_fusion.1
  27.9 2.1 fusion.116
  31.9 1.3 reshape.207
  33.2 2.0 reshape.208
  35.2 1.3 fusion.97
  39.8 2.4 multiply_convert_fusion
  42.9 0.8 copy-done.2
  45.9 1.3 add_convert_fusion
  48.3 1.1 copy.20
  49.9 1.9 reduce.2
  51.8 0.9 reshape.246
  52.6 9.5 %all-to-all-start = ((bf16[16,2,2250]{2,1,0:T(2,128)(2,1)}), bf16[16,2,2250]{2,1,0:T(2,128)(2,1)S(1)}, u32[]{:S(2)}, u32[]{:S(2)}) async-start(bf16[16,2,2250]{2,1,0:T(2,128)(2,1)} %reshape.246), calls=%async_computation | async-start | bytes 294912 | tf_op jit(solution)/shard_map/all_to_all | solution.py:132
  62.5 2.7 reshape.229
  65.2 2.0 slice.303
  67.2 5.4 %all-to-all-done = bf16[16,2,2250]{2,1,0:T(2,128)(2,1)S(1)} async-done(((bf16[16,2,2250]{2,1,0:T(2,128)(2,1)}), bf16[16,2,2250]{2,1,0:T(2,128)(2,1)S(1)}, u32[]{:S(2)}, u32[]{:S(2)}) %all-to-all-start) | async-done | bytes 144032 | tf_op jit(solution)/shard_map/all_to_all | solution.py:132
  73.0 1.1 bitcast_reduce_fusion
  74.9 1.3 copy.23
  76.2 12.8 %while.15 = (s32[]{:T(128)}, f32[16,100,45]{2,1,0:T(8,128)S(1)}, f32[16,100,45]{2,1,0:T(8,128)S(1)}, bf16[16,100,45]{1,2,0:T(8,128)(2,1)S(1)}, f32[16,100,45]{2,1,0:T(8,128)S(1)}, /*index=5*/s32[]{:T(128)}, s32[]{:T(128)}) while((s32[]{:T(128)}, f32[16,100,45]{2,1,0:T(8,128)S(1)}, f32[16,100,45]{2,1,0:T(8,128)S(1)}, ...), condition=%wide.region_1.2_spmd.clone, body=%wide.region_0.1_spmd.clone.sunk | while | flops 652503 | bytes 1521091 | solution.py:94
  89.7 1.6 multiply_reduce_fusion.2
  91.3 3.5 all-to-all-start.1
  94.9 1.7 fusion.115
  98.1 7.0 %all-to-all-done.1 = bf16[16,100,45]{1,2,0:T(8,128)(2,1)S(1)} async-done(((bf16[16,100,45]{1,2,0:T(8,128)(2,1)}), bf16[16,100,45]{1,2,0:T(8,128)(2,1)S(1)}, u32[]{:S(2)}, u32[]{:S(2)}) %all-to-all-start.1) | async-done | bytes 144032 | tf_op jit(solution)/shard_map/all_to_all | solution.py:142
  106.5 1.7 collective-permute-start.5
  111.5 3.0 collective-permute-start.6
  114.5 0.8 collective-permute-start.7
  115.3 0.9 fusion.118
  116.9 2.7 collective-permute-done.7
  120.4 0.9 copy-done.3
  123.6 0.8 copy-done.19
  126.8 0.9 copy-done.28
  127.8 170.7 %all-reduce.9.cloned.1.call-done = (f32[9,100,256]{2,1,0:T(8,128)}, f32[9,256,256]{2,1,0:T(8,128)}, f32[100,256]{1,0:T(8,128)}) async-done(((f32[9,100,256]{2,1,0:T(8,128)}, f32[9,256,256]{2,1,0:T(8,128)}, f32[100,256]{1,0:T(8,128)}), (f32[9,100,256]{2,1,0:T(8,128)}, f32[9,256,256]{2,1,0:T(8,128)}, f32[100,256]{1,0:T(8,128)})) %all-reduce.9.cloned.1.call-update) | async-done | bytes 3383312 | tf_op jit(solution)/shard_map/psum | solution.py:10
  299.2 66.2 %all-reduce.2 = (f32[32,256]{1,0:T(8,128)S(1)}, f32[]{:T(128)}) all-reduce(f32[32,256]{1,0:T(8,128)S(1)} %broadcast_multiply_fusion, f32[]{:T(128)} %get-tuple-element.167), channel_id=1, replica_groups=mesh['member'=16,'lat'=8,'lon'=2] {'member'}, use_global_device_ids=true, to_apply=%region_12.13 | all-reduce | flops 8193 | bytes 65544 | tf_op jit(solution)/shard_map/psum | solution.py:10
  365.4 66.1 %all-reduce = (f32[32,256]{1,0:T(8,128)S(1)}, f32[]{:T(128)}) all-reduce(f32[32,256]{1,0:T(8,128)S(1)} %get-tuple-element.116, f32[]{:T(128)} %get-tuple-element.117), channel_id=1, replica_groups=mesh['member'=16,'lat'=8,'lon'=2] {'lat','lon'}, use_global_device_ids=true, to_apply=%region_13.14 | all-reduce | flops 8193 | bytes 65544 | tf_op jit(solution)/shard_map/psum | solution.py:10
  434.1 45.4 %all-reduce.7.cloned.1.call-done = (f32[9,100,256]{2,1,0:T(8,128)}, f32[9,256,256]{2,1,0:T(8,128)}, f32[100,256]{1,0:T(8,128)}) async-done(((f32[9,100,256]{2,1,0:T(8,128)}, f32[9,256,256]{2,1,0:T(8,128)}, f32[100,256]{1,0:T(8,128)}), (f32[9,100,256]{2,1,0:T(8,128)}, f32[9,256,256]{2,1,0:T(8,128)}, f32[100,256]{1,0:T(8,128)})) %all-reduce.7.cloned.1.call-update) | async-done | bytes 3383312 | tf_op jit(solution)/shard_map/psum | solution.py:10
  479.6 1.7 multiply_reduce_fusion.3
  481.9 1.6 broadcast_divide_fusion.2
  483.5 2.9 multiply_reduce_fusion
  487.1 1.6 broadcast_divide_fusion
  488.7 0.8 multiply_reduce_fusion.1
  490.3 1.0 broadcast_divide_fusion.1
  (228 shorter events, 38.3 us)
Async XLA Ops:
  7.2 40.8 %copy-start = (bf16[100,256]{1,0:T(8,128)(2,1)S(1)}, bf16[100,256]{1,0:T(8,128)(2,1)}, u32[]{:S(2)}) copy-start(bf16[100,256]{1,0:T(8,128)(2,1)} %param.16) | copy-start | bytes 153604
  7.2 19.5 %copy-start.27 = (bf16[100,2,360]{2,1,0:T(2,128)(2,1)S(1)}, bf16[100,2,360]{2,1,0:T(2,128)(2,1)}, u32[]{:S(2)}) copy-start(bf16[100,2,360]{2,1,0:T(2,128)(2,1)} %param.10) | copy-start | bytes 432004
  7.2 4.9 collective-permute-start
  7.2 4.8 collective-permute-start.1
  13.4 8.9 %collective-permute-start.2 = (bf16[100,6,2]{2,1,0:T(8,128)(2,1)S(1)}, bf16[100,6,2]{2,1,0:T(8,128)(2,1)S(1)}, u32[]{:S(2)}, u32[]{:S(2)}) collective-permute-start(bf16[100,6,2]{2,1,0:T(8,128)(2,1)S(1)} %get-tuple-element.163), channel_id=1, source_target_pairs={{0,1},{1,0},{2,3},{3,2},{4,5},{5,4},{6,7},{7,6},{8,9},{9,8},{10,11... | collective-permute-start | bytes 7208 | tf_op jit(solution)/shard_map/ppermute | solution.py:19
  16.5 10.1 %collective-permute-start.3 = (bf16[100,6,2]{2,1,0:T(8,128)(2,1)S(1)}, bf16[100,6,2]{2,1,0:T(8,128)(2,1)S(1)}, u32[]{:S(2)}, u32[]{:S(2)}) collective-permute-start(bf16[100,6,2]{2,1,0:T(8,128)(2,1)S(1)} %get-tuple-element.164), channel_id=1, source_target_pairs={{1,0},{0,1},{3,2},{2,3},{5,4},{4,5},{7,6},{6,7},{9,8},{8,9},{11,10... | collective-permute-start | bytes 7208 | tf_op jit(solution)/shard_map/ppermute | solution.py:22
  35.2 1.3 copy-start.29
  38.8 1.0 copy-start.30
  42.5 1.3 copy-start.2
  42.8 1.4 copy-start.17
  42.8 1.4 copy-start.23
  42.8 1.4 copy-start.15
  42.8 1.7 copy-start.13
  42.8 2.2 copy-start.9
  42.9 2.5 copy-start.7
  42.9 2.7 copy-start.5
  42.9 3.0 copy-start.11
  42.9 3.0 copy-start.25
  47.3 0.7 copy-start.21
  47.3 14.9 %copy-start.32 = (s32[2,360]{1,0:T(2,128)S(1)}, s32[2,360]{1,0:T(2,128)}, u32[]{:S(2)}) copy-start(s32[2,360]{1,0:T(2,128)} %param.12) | copy-start | bytes 8644
  47.3 14.9 %copy-start.31 = (bf16[100,2,360]{2,1,0:T(2,128)(2,1)S(1)}, bf16[100,2,360]{2,1,0:T(2,128)(2,1)}, u32[]{:S(2)}) copy-start(bf16[100,2,360]{2,1,0:T(2,128)(2,1)} %param.11) | copy-start | bytes 432004
  52.6 20.0 %all-to-all-start = ((bf16[16,2,2250]{2,1,0:T(2,128)(2,1)}), bf16[16,2,2250]{2,1,0:T(2,128)(2,1)S(1)}, u32[]{:S(2)}, u32[]{:S(2)}) async-start(bf16[16,2,2250]{2,1,0:T(2,128)(2,1)} %reshape.246), calls=%async_computation | async-start | bytes 294912 | tf_op jit(solution)/shard_map/all_to_all | solution.py:132
  91.3 13.7 %all-to-all-start.1 = ((bf16[16,100,45]{1,2,0:T(8,128)(2,1)}), bf16[16,100,45]{1,2,0:T(8,128)(2,1)S(1)}, u32[]{:S(2)}, u32[]{:S(2)}) async-start(bf16[16,100,45]{1,2,0:T(8,128)(2,1)} %get-tuple-element.168), calls=%async_computation.1 | async-start | bytes 393216 | tf_op jit(solution)/shard_map/all_to_all | solution.py:142
  94.9 203.6 %all-reduce.9.cloned.1.call-start = ((), (), s32[]{:S(2)}) async-start(), calls=%async_computation.3 | async-start | bytes 6848512 | tf_op jit(solution)/shard_map/psum | solution.py:10
  96.8 8.3 %copy-start.34 = (f32[256,720]{0,1:T(8,128)S(1)}, f32[256,720]{0,1:T(8,128)}, u32[]{:S(2)}) copy-start(f32[256,720]{0,1:T(8,128)} %get-tuple-element.170) | copy-start | bytes 2211844
  105.2 1.0 copy-start.24
  105.7 2.6 copy-start.18
  105.7 2.9 copy-start.16
  106.5 2.5 copy-start.14
  106.5 5.0 collective-permute-start.4
  106.5 2.7 copy-start.12
  106.5 4.9 collective-permute-start.5
  108.6 1.0 copy-start.10
  108.9 1.0 copy-start.8
  109.3 1.0 copy-start.6
  109.6 1.0 copy-start.26
  110.3 5.0 %copy-start.22 = (bf16[256,720]{0,1:T(8,128)(2,1)S(1)}, bf16[256,720]{0,1:T(8,128)(2,1)}, u32[]{:S(2)}) copy-start(bf16[256,720]{0,1:T(8,128)(2,1)} %copy-done.21) | copy-start | bytes 1105924
  111.0 9.4 %copy-start.20 = (f32[9,256,256]{2,1,0:T(8,128)}, f32[9,256,256]{2,1,0:T(8,128)S(1)}, u32[]{:S(2)}) copy-start(f32[9,256,256]{2,1,0:T(8,128)S(1)} %fusion.19) | copy-start | bytes 7077892
  111.5 5.4 %collective-permute-start.6 = (bf16[256,4,1]{0,2,1:T(2,128)(2,1)S(1)}, bf16[256,4,1]{0,2,1:T(2,128)(2,1)S(1)}, u32[]{:S(2)}, u32[]{:S(2)}) collective-permute-start(bf16[256,4,1]{0,2,1:T(2,128)(2,1)S(1)} %get-tuple-element.143), channel_id=1, source_target_pairs={{0,1},{1,0},{2,3},{3,2},{4,5},{5,4},{6,7},{7,6},{8,9},{9,8},{10,11... | collective-permute-start | bytes 6152 | tf_op jit(solution)/shard_map/ppermute | solution.py:19
  114.5 5.1 %collective-permute-start.7 = (bf16[256,4,1]{0,2,1:T(2,128)(2,1)S(1)}, bf16[256,4,1]{0,2,1:T(2,128)(2,1)S(1)}, u32[]{:S(2)}, u32[]{:S(2)}) collective-permute-start(bf16[256,4,1]{0,2,1:T(2,128)(2,1)S(1)} %get-tuple-element.144), channel_id=1, source_target_pairs={{1,0},{0,1},{3,2},{2,3},{5,4},{4,5},{7,6},{6,7},{9,8},{8,9},{11,10... | collective-permute-start | bytes 6152 | tf_op jit(solution)/shard_map/ppermute | solution.py:22
  120.0 1.3 copy-start.3
  123.3 1.1 copy-start.19
  126.8 0.9 copy-start.28
  127.7 351.8 %all-reduce.7.cloned.1.call-start = ((), (), s32[]{:S(2)}) async-start(), calls=%async_computation.2 | async-start | bytes 6848512 | tf_op jit(solution)/shard_map/psum | solution.py:10
  298.5 0.7 copy-start.33
  479.6 7.5 %copy-start.1 = (f32[9,256,256]{2,1,0:T(8,128)S(1)}, f32[9,256,256]{2,1,0:T(8,128)}, u32[]{:S(2)}) copy-start(f32[9,256,256]{2,1,0:T(8,128)} %get-tuple-element.114) | copy-start | bytes 7077892
  487.1 1.6 copy-start.4
Sparse Core Ops, SparseCore 0:
  127.8 170.6 all-reduce.8
  301.4 178.1 all-reduce.6
